TPU v7x, 128 devices: a whole 4x4x4 slice. The times are simulated.
128 devices in a mesh: group: 4 (over z_lo, core), dp: 2 (over z_hi), tensor: 16 (over x, y).
Axes of the slice: x: 4, y: 4, z: 4 (z_hi: 2, z_lo: 2; z = z_hi * 2 + z_lo), core: 2. Of those that a mesh axis runs over, the one named last changes fastest.
Arguments:
- tokens: bfloat16 [2048, 8, 2048], P('tensor', ('group', 'dp')), may hold values from -6 to 6
- cotangent: bfloat16 [2048, 8, 2048], P('tensor', ('group', 'dp')), may hold values from -6 to 6
- lengths: int32 [8], replicated, may hold values from 1 to 2048, 9830 in all
- ln1_gain: float32 [2048], replicated, may hold values from 0.25 to 1.75
- ln1_bias: float32 [2048], replicated, may hold values from -1.75 to 1.75
- w_qkv: bfloat16 [2048, 3, 16, 128], P(None, None, 'tensor'), may hold values from -0.125 to 0.125
- b_qv: float32 [2, 2048], P(None, 'tensor'), may hold values from -1.75 to 1.75
- w_o: bfloat16 [16, 128, 2048], P('tensor'), may hold values from -0.75 to 0.75
- b_o: float32 [2048], replicated, may hold values from -1.75 to 1.75
- ln2_gain: float32 [2048], replicated, may hold values from 0.25 to 1.75
- ln2_bias: float32 [2048], replicated, may hold values from -1.75 to 1.75
- w_in: bfloat16 [2048, 8192], P(None, 'tensor'), may hold values from -0.125 to 0.125
- b_in: float32 [8192], P('tensor'), may hold values from -1.75 to 1.75
- w_out: bfloat16 [8192, 2048], P('tensor'), may hold values from -0.0625 to 0.0625
- b_out: float32 [2048], replicated, may hold values from -1.75 to 1.75
Outputs:
- output: bfloat16 [2048, 8, 2048], P('tensor', ('group', 'dp'))
- input_grad: bfloat16 [2048, 8, 2048], P('tensor', ('group', 'dp'))
- d_ln1_gain: float32 [2048], P(('group', 'dp', 'tensor'))
- d_ln1_bias: float32 [2048], P(('group', 'dp', 'tensor'))
- d_w_qkv: float32 [2048, 3, 16, 128], P(('group', 'dp'), None, 'tensor')
- d_b_qv: float32 [2, 2048], P(None, ('group', 'dp', 'tensor'))
- d_w_o: float32 [16, 128, 2048], P('tensor', None, ('group', 'dp'))
- d_b_o: float32 [2048], P(('group', 'dp', 'tensor'))
- d_ln2_gain: float32 [2048], P(('group', 'dp', 'tensor'))
- d_ln2_bias: float32 [2048], P(('group', 'dp', 'tensor'))
- d_w_in: float32 [2048, 8192], P(('group', 'dp'), 'tensor')
- d_b_in: float32 [8192], P(('group', 'dp', 'tensor'))
- d_w_out: float32 [8192, 2048], P('tensor', ('group', 'dp'))
- d_b_out: float32 [2048], P(('group', 'dp', 'tensor'))
Inputs may be any that keep to these rules, and one draw needn't show every extreme that they name: The true lengths of the 8 sequences sum to 9830.
All inputs are finite; a program needn't handle non-finite values.
Results may differ from a plain program's by a relative error of at most 0.02.
Values may be sent and summed in bfloat16 or wider, within the bound.
No kernel may reach another device: no remote copies, remote signals or barrier semaphores. Data moves between devices by JAX's collectives and lax.ppermute only.
A program may use at most 192 MiB of HBM per device.

v0:
```python
from functools import partial
import math
import jax
import jax.numpy as jnp
from jax import lax
from jax.sharding import PartitionSpec as P

EPS = 1e-05
NEGATIVE = -1e30


def layer_norm(value, gain, shift):
    mean = jnp.mean(value, axis=-1, keepdims=True)
    centred = value - mean
    spread = jnp.mean(centred * centred, axis=-1, keepdims=True)
    return centred * lax.rsqrt(spread + EPS) * gain + shift


def gelu_tanh(value):
    return jax.nn.gelu(value, approximate=True)


def block_scores(rows_query, key_rows, first, length, score_scale):
    count = rows_query.shape[0]
    key_pos = jnp.arange(key_rows.shape[0], dtype=jnp.int32)
    query_pos = first + jnp.arange(count, dtype=jnp.int32)
    valid = (key_pos[None, :] <= query_pos[:, None]) & (key_pos[None, :] < length)
    scores = (
        lax.dot_general(
            rows_query, key_rows, (((1,), (1,)), ((), ())), preferred_element_type=jnp.float32
        )
        * score_scale
    )
    return (jnp.where(valid, scores, NEGATIVE), valid)


def attend_forward(item, block_rows, score_scale):
    query, key_rows, value_rows, length = item
    outputs = []
    log_parts = []
    for first in range(0, query.shape[0], block_rows):
        rows_query = query[first : first + block_rows]
        scores, valid = block_scores(rows_query, key_rows, first, length, score_scale)
        peak = jnp.max(scores, axis=-1, keepdims=True)
        expo = jnp.exp(scores - peak)
        weight_sum = jnp.sum(expo, axis=-1, keepdims=True)
        probs = (expo / weight_sum).astype(jnp.bfloat16)
        outputs.append(
            jnp.dot(probs, value_rows, preferred_element_type=jnp.float32).astype(jnp.bfloat16)
        )
        log_parts.append((peak + jnp.log(weight_sum))[:, 0])
    return (jnp.concatenate(outputs, 0), jnp.concatenate(log_parts, 0))


def attend_backward(item, block_rows, score_scale):
    query, key_rows, value_rows, length, grad_out, log_sums = item
    key_grad = jnp.zeros(key_rows.shape, jnp.float32)
    value_grad = jnp.zeros(value_rows.shape, jnp.float32)
    query_parts = []
    for first in range(0, query.shape[0], block_rows):
        rows_query = query[first : first + block_rows]
        scores, valid = block_scores(rows_query, key_rows, first, length, score_scale)
        probs = jnp.where(valid, jnp.exp(scores - log_sums[first : first + block_rows, None]), 0.0)
        grad_rows = grad_out[first : first + block_rows]
        probs_grad = lax.dot_general(
            grad_rows, value_rows, (((1,), (1,)), ((), ())), preferred_element_type=jnp.float32
        )
        inner = jnp.sum(probs * probs_grad, axis=-1, keepdims=True)
        score_grad = (probs * (probs_grad - inner)).astype(jnp.bfloat16)
        query_parts.append(
            jnp.dot(score_grad, key_rows, preferred_element_type=jnp.float32) * score_scale
        )
        key_grad = (
            key_grad
            + lax.dot_general(
                score_grad, rows_query, (((0,), (0,)), ((), ())), preferred_element_type=jnp.float32
            )
            * score_scale
        )
        value_grad = value_grad + lax.dot_general(
            probs.astype(jnp.bfloat16),
            grad_rows,
            (((0,), (0,)), ((), ())),
            preferred_element_type=jnp.float32,
        )
    return (
        jnp.concatenate(query_parts, 0).astype(jnp.bfloat16),
        key_grad.astype(jnp.bfloat16),
        value_grad.astype(jnp.bfloat16),
    )


def shards(
    tokens,
    cotangent,
    lengths,
    ln1_gain,
    ln1_bias,
    w_qkv,
    b_qv,
    w_o,
    b_o,
    ln2_gain,
    ln2_bias,
    w_in,
    b_in,
    w_out,
    b_out,
):
    row_count, seq_count, model_width = tokens.shape
    tensor_count = lax.axis_size("tensor")
    tensor_rank = lax.axis_index("tensor")
    seq_total = row_count * tensor_count
    local_heads = w_qkv.shape[2]
    head_size = w_qkv.shape[3]
    local_width = local_heads * head_size
    hidden = w_in.shape[1]
    block_rows = min(512, seq_total)
    score_scale = 1.0 / math.sqrt(head_size)
    group_count = lax.axis_size("group")
    group_rank = lax.axis_index("group")
    member = group_rank * lax.axis_size("dp") + lax.axis_index("dp")
    seq_lengths = lax.dynamic_slice_in_dim(lengths, member * seq_count, seq_count, 0)
    group_totals = jnp.sum(lengths.reshape(group_count, -1), axis=1).astype(jnp.float32)
    factor = (
        group_count
        * lax.dynamic_index_in_dim(group_totals, group_rank, 0, keepdims=False)
        / jnp.sum(group_totals)
    )
    inputs = tokens.astype(jnp.float32)
    normed_low = layer_norm(inputs, ln1_gain, ln1_bias).astype(jnp.bfloat16)
    normed_full = lax.all_gather(normed_low, "tensor", axis=0, tiled=True)
    joint_weight = w_qkv.reshape(model_width, 3 * local_width)
    projected = jnp.dot(
        normed_full.reshape(seq_total * seq_count, model_width),
        joint_weight,
        preferred_element_type=jnp.float32,
    )
    projected = projected.reshape(seq_total, seq_count, 3, local_width)
    query = (projected[:, :, 0] + b_qv[0]).astype(jnp.bfloat16)
    keys = projected[:, :, 1].astype(jnp.bfloat16)
    values = (projected[:, :, 2] + b_qv[1]).astype(jnp.bfloat16)

    def per_item(array):
        shaped = array.reshape(seq_total, seq_count, local_heads, head_size)
        return jnp.transpose(shaped, (1, 2, 0, 3)).reshape(
            seq_count * local_heads, seq_total, head_size
        )

    def per_row(array):
        shaped = array.reshape(seq_count, local_heads, seq_total, head_size)
        return jnp.transpose(shaped, (2, 0, 1, 3)).reshape(seq_total, seq_count, local_width)

    query_items = per_item(query)
    key_items = per_item(keys)
    value_items = per_item(values)
    item_lengths = jnp.repeat(seq_lengths, local_heads)
    heads_out, log_sums = lax.map(
        partial(attend_forward, block_rows=block_rows, score_scale=score_scale),
        (query_items, key_items, value_items, item_lengths),
    )
    attended = per_row(heads_out)
    out_weight = w_o.reshape(local_width, model_width)
    piece = attended
    attention = (
        lax.psum_scatter(
            jnp.einsum("rse,ed->rsd", piece, out_weight, preferred_element_type=jnp.float32),
            "tensor",
            scatter_dimension=0,
            tiled=True,
        )
        + b_o
    )
    middle = inputs + attention
    second_low = layer_norm(middle, ln2_gain, ln2_bias).astype(jnp.bfloat16)
    second_full = lax.all_gather(second_low, "tensor", axis=0, tiled=True)
    pre_act = (
        jnp.dot(
            second_full.reshape(seq_total * seq_count, model_width),
            w_in,
            preferred_element_type=jnp.float32,
        )
        + b_in
    )
    activated = gelu_tanh(pre_act).astype(jnp.bfloat16).reshape(seq_total, seq_count, hidden)
    piece = activated
    feed = (
        lax.psum_scatter(
            jnp.einsum("rsf,fd->rsd", piece, w_out, preferred_element_type=jnp.float32).astype(
                jnp.bfloat16
            ),
            "tensor",
            scatter_dimension=0,
            tiled=True,
        ).astype(jnp.float32)
        + b_out
    )
    output = (middle + feed).astype(jnp.bfloat16)
    positions = tensor_rank * row_count + jnp.arange(row_count, dtype=jnp.int32)
    live = positions[:, None] < seq_lengths[None, :]
    upstream = jnp.where(live[:, :, None], cotangent, jnp.zeros_like(cotangent))
    piece = lax.all_gather(upstream, "tensor", axis=0, tiled=True)
    weight_grad = jnp.einsum("rsf,rsd->fd", activated, piece, preferred_element_type=jnp.float32)
    part = jnp.einsum("rsd,fd->rsf", piece, w_out, preferred_element_type=jnp.float32)
    act_grad = part
    grad_w_out = weight_grad
    gelu_back = jax.vjp(gelu_tanh, pre_act)[1]
    pre_low = gelu_back(act_grad.reshape(seq_total * seq_count, hidden))[0].astype(jnp.bfloat16)
    grad_b_in = jnp.sum(pre_low, axis=0, dtype=jnp.float32)
    grad_w_in = jnp.einsum(
        "rd,rf->df",
        second_full.reshape(seq_total * seq_count, model_width),
        pre_low,
        preferred_element_type=jnp.float32,
    )
    pre_rows = pre_low.reshape(seq_total, seq_count, hidden)
    piece = pre_rows
    second_grad = lax.psum_scatter(
        jnp.einsum("rsf,df->rsd", piece, w_in, preferred_element_type=jnp.float32),
        "tensor",
        scatter_dimension=0,
        tiled=True,
    )
    norm_two_back = jax.vjp(layer_norm, middle, ln2_gain, ln2_bias)[1]
    middle_part, grad_ln2_gain, grad_ln2_bias = norm_two_back(second_grad)
    middle_grad = upstream.astype(jnp.float32) + middle_part
    branch_low = middle_grad.astype(jnp.bfloat16)
    grad_b_o = jnp.sum(branch_low, axis=(0, 1), dtype=jnp.float32)
    grad_b_out = jnp.sum(upstream, axis=(0, 1), dtype=jnp.float32)
    piece = lax.all_gather(branch_low, "tensor", axis=0, tiled=True)
    weight_grad = jnp.einsum("rse,rsd->ed", attended, piece, preferred_element_type=jnp.float32)
    part = jnp.einsum("rsd,ed->rse", piece, out_weight, preferred_element_type=jnp.float32)
    head_items = per_item(part.astype(jnp.bfloat16))
    grads_query, grads_keys, grads_values = lax.map(
        partial(attend_backward, block_rows=block_rows, score_scale=score_scale),
        (query_items, key_items, value_items, item_lengths, head_items, log_sums),
    )
    joint_grad = jnp.stack(
        (per_row(grads_query), per_row(grads_keys), per_row(grads_values)), axis=2
    )
    grad_b_qv = jnp.sum(joint_grad[:, :, 0::2], axis=(0, 1), dtype=jnp.float32)
    joint_rows = joint_grad.reshape(seq_total, seq_count, 3 * local_width)
    grad_w_qkv = jnp.einsum(
        "rd,rc->dc",
        normed_full.reshape(seq_total * seq_count, model_width),
        joint_rows.reshape(seq_total * seq_count, 3 * local_width),
        preferred_element_type=jnp.float32,
    )
    piece = joint_rows
    normed_grad = lax.psum_scatter(
        jnp.einsum("rsc,dc->rsd", piece, joint_weight, preferred_element_type=jnp.float32).astype(
            jnp.bfloat16
        ),
        "tensor",
        scatter_dimension=0,
        tiled=True,
    ).astype(jnp.float32)
    norm_one_back = jax.vjp(layer_norm, inputs, ln1_gain, ln1_bias)[1]
    input_part, grad_ln1_gain, grad_ln1_bias = norm_one_back(normed_grad)
    input_grad = (middle_grad + input_part).astype(jnp.bfloat16)
    summed = (
        halving_sum(grad_w_qkv.reshape(model_width, 3, local_heads, head_size) * factor, 0),
        halving_sum(weight_grad.reshape(local_heads, head_size, model_width) * factor, 2),
        halving_sum(grad_w_in * factor, 0),
        halving_sum(grad_w_out * factor, 1),
    )
    in_full = lax.dynamic_update_slice_in_dim(
        jnp.zeros((hidden * tensor_count,), jnp.float32), grad_b_in, tensor_rank * hidden, 0
    )
    joint_full = lax.dynamic_update_slice_in_dim(
        jnp.zeros((2, local_width * tensor_count), jnp.float32),
        grad_b_qv,
        tensor_rank * local_width,
        1,
    )
    shard_count = group_count * lax.axis_size("dp")
    vectors = (
        grad_ln1_gain,
        grad_ln1_bias,
        grad_b_o,
        grad_ln2_gain,
        grad_ln2_bias,
        grad_b_out,
        joint_full[0],
        joint_full[1],
        in_full,
    )
    pieces = [
        jnp.transpose((item * factor).reshape(shard_count, tensor_count, -1), (1, 0, 2))
        for item in vectors
    ]
    widths = [piece.shape[2] for piece in pieces]
    packed = jnp.concatenate(pieces, 2)
    packed = halving_steps(
        packed,
        0,
        [
            ("tensor", tensor_count, 8),
            ("tensor", tensor_count, 4),
            ("tensor", tensor_count, 2),
            ("tensor", tensor_count, 1),
        ],
    )
    packed = halving_steps(
        packed,
        1,
        [("group", group_count, 2), ("group", group_count, 1), ("dp", lax.axis_size("dp"), 1)],
    )
    flat = packed.reshape(-1)
    parts = []
    offset = 0
    for width in widths:
        parts.append(flat[offset : offset + width])
        offset += width
    return (
        output,
        input_grad,
        parts[0],
        parts[1],
        summed[0],
        jnp.stack((parts[6], parts[7])),
        summed[1],
        parts[2],
        parts[3],
        parts[4],
        summed[2],
        parts[8],
        summed[3],
        parts[5],
    )


def halving_steps(value, dim, steps, send_type=None):
    for axis, size, bit in steps:
        half = value.shape[dim] // 2
        low_half = lax.slice_in_dim(value, 0, half, axis=dim)
        high_half = lax.slice_in_dim(value, half, 2 * half, axis=dim)
        upper = lax.axis_index(axis) // bit % 2 == 1
        keep = jnp.where(upper, high_half, low_half)
        send = jnp.where(upper, low_half, high_half)
        if send_type is not None:
            send = send.astype(send_type)
        got = lax.ppermute(send, axis, [(i, i ^ bit) for i in range(size)])
        value = keep + got.astype(keep.dtype)
    return value


def halving_sum(value, dim):
    shape = value.shape
    groups = lax.axis_size("group")
    dps = lax.axis_size("dp")
    split = shape[:dim] + (groups * dps, shape[dim] // (groups * dps)) + shape[dim + 1 :]
    value = value.reshape(split)
    value = halving_steps(
        value, dim, [("group", groups, 2), ("group", groups, 1), ("dp", dps, 1)], jnp.bfloat16
    )
    return value.reshape(shape[:dim] + (shape[dim] // (groups * dps),) + shape[dim + 1 :])


def solution(mesh):
    in_specs = (
        P("tensor", ("group", "dp"), None),
        P("tensor", ("group", "dp"), None),
        P(),
        P(),
        P(),
        P(None, None, "tensor", None),
        P(None, "tensor"),
        P("tensor", None, None),
        P(),
        P(),
        P(),
        P(None, "tensor"),
        P("tensor"),
        P("tensor", None),
        P(),
    )
    out_specs = (
        P("tensor", ("group", "dp"), None),
        P("tensor", ("group", "dp"), None),
        P(("group", "dp", "tensor")),
        P(("group", "dp", "tensor")),
        P(("group", "dp"), None, "tensor", None),
        P(None, ("group", "dp", "tensor")),
        P("tensor", None, ("group", "dp")),
        P(("group", "dp", "tensor")),
        P(("group", "dp", "tensor")),
        P(("group", "dp", "tensor")),
        P(("group", "dp"), "tensor"),
        P(("group", "dp", "tensor")),
        P("tensor", ("group", "dp")),
        P(("group", "dp", "tensor")),
    )
    return jax.shard_map(shards, mesh=mesh, in_specs=in_specs, out_specs=out_specs, check_vma=False)
```

profile of v0, /device:TPU:0, one launch (start us, length us, event | category | flops | bytes accessed | tf_op | source)
XLA Modules:
  0.0 947.7 jit_solution(5569445801283736321)
XLA Ops:
  10.5 2.3 fusion.74
  12.8 2.7 copy.44
  16.8 69.2 %all-gather.5.cloned.1.call-done = bf16[2048,1,2048]{2,0,1:T(8,128)(2,1)} async-done(((bf16[128,1,2048]{2,0,1:T(8,128)(2,1)}), bf16[2048,1,2048]{2,0,1:T(8,128)(2,1)}) %all-gather.5.cloned.1.call-update) | async-done | bytes 8388624 | tf_op jit(solution)/shard_map/all_gather | solution.py:132
  86.0 7.4 fusion.33
  94.7 2.9 fusion.119
  97.7 3.3 fusion.122
  101.0 4.0 online-softmax.3
  106.0 4.6 fusion.121
  110.6 4.0 online-softmax.2
  115.5 4.6 fusion.120
  120.1 4.0 online-softmax.1
  125.2 4.2 online-softmax
  130.4 8.1 convolution_bitcast_fusion.1
  138.6 110.4 %reduce-scatter.5.cloned.1.call-done = f32[128,1,2048]{2,0,1:T(8,128)} async-done(((f32[2048,1,2048]{2,0,1:T(8,128)}), f32[128,1,2048]{2,0,1:T(8,128)}) %reduce-scatter.5.cloned.1.call-update) | async-done | bytes 1048592 | tf_op jit(solution)/shard_map/reduce_scatter | solution.py:166
  252.6 2.0 convert_reduce_fusion.4
  254.8 67.5 %all-gather.7.cloned.1.call-done = bf16[2048,1,2048]{2,0,1:T(8,128)(2,1)} async-done(((bf16[128,1,2048]{2,0,1:T(8,128)(2,1)}), bf16[2048,1,2048]{2,0,1:T(8,128)(2,1)}) %all-gather.7.cloned.1.call-update) | async-done | bytes 8388624 | tf_op jit(solution)/shard_map/all_gather | solution.py:176
  322.3 10.5 %fusion.10 = f32[2048,512]{1,0:T(8,128)} fusion(bf16[2048,512]{1,0:T(8,128)(2,1)} %param.26, bf16[2048,1,2048]{2,0,1:T(8,128)(2,1)} %all-gather.7.cloned.1.call-done), kind=kOutput, calls=%fused_computation.12 | convolution fusion | flops 4294967296 | bytes 14680064 | tf_op jit(solution)/shard_map/dot_general | solution.py:178
  332.8 62.4 %all-gather.9.cloned.1.call-done = bf16[2048,1,2048]{2,0,1:T(8,128)(2,1)} async-done(((bf16[128,1,2048]{2,0,1:T(8,128)(2,1)}), bf16[2048,1,2048]{2,0,1:T(8,128)(2,1)}) %all-gather.9.cloned.1.call-update) | async-done | bytes 8388624 | tf_op jit(solution)/shard_map/all_gather | solution.py:202
  395.2 12.7 %convert_reduce_fusion = (f32[512]{0:T(512)}, bf16[2048,512]{1,0:T(8,128)(2,1)S(1)}) fusion(f32[2048,512]{1,0:T(8,128)} %fusion.10, f32[512]{0:T(512)S(1)} %copy-done.72, bf16[512,2048]{1,0:T(8,128)(2,1)S(1)} %copy-done, bf16[2048,1,2048]{2,0,1:T(8,128)(2,1)} %all-gather.9.cloned.1.call-done), kind=kOutput, calls=%fused_computation.29 | convolution fusion | flops 4319084032 | bytes 16781312 | tf_op jit(solution)/shard_map/rsd,fd->rsf/dot_general | solution.py:204
  409.3 8.3 convolution_bitcast_fusion
  417.7 10.2 %convert_bitcast_fusion.1 = bf16[2048,1,2048]{2,0,1:T(8,128)(2,1)} fusion(bf16[512,2048]{1,0:T(8,128)(2,1)S(1)} %copy-done, f32[2048,512]{1,0:T(8,128)} %fusion.10, f32[512]{0:T(512)S(1)} %copy-done.72), kind=kOutput, calls=%fused_computation.19 | convolution fusion | flops 4309647360 | bytes 14682112 | tf_op jit(solution)/shard_map/rsf,fd->rsd/dot_general | solution.py:189
  428.0 100.0 %reduce-scatter.9.cloned.1.call-done = f32[128,1,2048]{2,0,1:T(8,128)} async-done(((f32[2048,1,2048]{2,0,1:T(8,128)}), f32[128,1,2048]{2,0,1:T(8,128)}) %reduce-scatter.9.cloned.1.call-update) | async-done | bytes 1048592 | tf_op jit(solution)/shard_map/reduce_scatter | solution.py:218
  528.0 2.2 multiply_reduce_fusion.4
  530.2 85.8 %reduce-scatter.7.cloned.1.call-done = bf16[128,1,2048]{2,0,1:T(8,128)(2,1)} async-done(((bf16[2048,1,2048]{2,0,1:T(8,128)(2,1)}), bf16[128,1,2048]{2,0,1:T(8,128)(2,1)}) %reduce-scatter.7.cloned.1.call-update) | async-done | bytes 524304 | tf_op jit(solution)/shard_map/reduce_scatter | solution.py:188
  616.0 2.6 fusion.115
  619.9 3.0 exponential_reduce_fusion
  628.1 61.8 %all-gather.11.cloned.1.call-done = bf16[2048,1,2048]{2,0,1:T(8,128)(2,1)} async-done(((bf16[128,1,2048]{2,0,1:T(8,128)(2,1)}), bf16[2048,1,2048]{2,0,1:T(8,128)(2,1)}) %all-gather.11.cloned.1.call-update) | async-done | bytes 8388624 | tf_op jit(solution)/shard_map/all_gather | solution.py:230
  689.9 5.7 fusion.45
  695.6 2.7 fusion.96
  698.4 2.8 fusion.99
  701.2 2.8 fusion.102
  704.1 1.9 fusion.55
  707.7 10.2 %multiply_reduce_fusion = (f32[512]{0:T(512)}, f32[512]{0:T(512)}, f32[512]{0:T(512)}, f32[512]{0:T(512)}, f32[512,2048]{1,0:T(8,128)}) fusion(f32[512,2048]{1,0:T(8,128)S(1)} %copy-done.2, f32[512]{0:T(512)S(1)} %get-tuple-element.117, pred[2048]{0:T(1024)(128)(4,1)S(1)} %iota_compare_fusion.4, s32[512]{0:T(512)S(1)} %iota_add_fusion, ...), kind=kOutput, calls=%fused_computation.31 | convolution fusion | flops 293599232 | bytes 34234368 | tf_op jit(solution)/shard_map/while/body/eval_jaxpr/dot_general | solution.py:65
  717.9 9.4 multiply_convert_fusion
  727.4 2.0 fusion.72
  730.2 1.7 convolution_add_fusion.2
  732.0 1.7 convolution_add_fusion.1
  733.7 2.0 fusion.50
  735.8 2.4 multiply_convert_fusion.1
  742.9 1.6 copy.53
  744.5 9.7 %convert_bitcast_fusion = bf16[2048,1,2048]{2,0,1:T(8,128)(2,1)} fusion(bf16[2048,384]{0,1:T(8,128)(2,1)} %bitcast.201, bf16[2048,384]{0,1:T(8,128)(2,1)} %bitcast.202), kind=kOutput, calls=%fused_computation.18 | convolution fusion | flops 3225419776 | bytes 11534336 | tf_op jit(solution)/shard_map/rsc,dc->rsd/dot_general | solution.py:251
  757.6 8.7 fusion.27
  766.3 2.0 copy.76
  768.3 7.1 fusion.30
  780.3 1.6 select_convert_fusion
  783.2 2.8 slice_select_fusion
  786.0 17.0 %collective-permute-done.13 = bf16[4,256,512]{2,1,0:T(8,128)(2,1)S(1)} collective-permute-done((bf16[4,256,512]{2,1,0:T(8,128)(2,1)}, bf16[4,256,512]{2,1,0:T(8,128)(2,1)S(1)}, u32[]{:S(2)}, u32[]{:S(2)}) %collective-permute-start.13) | collective-permute-done | bytes 1048608 | tf_op jit(solution)/shard_map/ppermute | solution.py:343
  803.6 20.9 %collective-permute-done.16 = bf16[512,4,256]{2,0,1:T(8,128)(2,1)} collective-permute-done((bf16[512,4,256]{2,0,1:T(8,128)(2,1)}, bf16[512,4,256]{2,0,1:T(8,128)(2,1)}, u32[]{:S(2)}, u32[]{:S(2)}) %collective-permute-start.16) | collective-permute-done | bytes 1048608 | tf_op jit(solution)/shard_map/ppermute | solution.py:343
  824.4 2.0 convert_add_fusion
  827.0 3.2 collective-permute-start.15
  831.2 1.6 collective-permute-start.18
  834.3 3.4 collective-permute-done.15
  838.6 4.3 collective-permute-done.18
  846.7 4.7 fusion.42
  852.0 1.6 collective-permute-start.10
  853.7 7.0 fusion.36
  864.6 2.9 collective-permute-start.12
  877.2 3.2 collective-permute-start
  880.4 25.4 %collective-permute-done.7 = bf16[4,256,3,1,128]{4,3,2,1,0:T(2,128)(2,1)} collective-permute-done((bf16[4,256,3,1,128]{4,3,2,1,0:T(2,128)(2,1)S(1)}, bf16[4,256,3,1,128]{4,3,2,1,0:T(2,128)(2,1)}, u32[]{:S(2)}, u32[]{:S(2)}) %collective-permute-start.7) | collective-permute-done | bytes 786464 | tf_op jit(solution)/shard_map/ppermute | solution.py:343
  905.8 4.3 copy_add_fusion
  912.6 1.6 collective-permute-done.1
  914.3 3.0 collective-permute-start.2
  923.8 7.1 collective-permute-done.9
  935.7 3.1 collective-permute-done.6
  (309 shorter events, 74.6 us)
Async XLA Ops:
  7.2 388.0 %copy-start = (bf16[512,2048]{1,0:T(8,128)(2,1)S(1)}, bf16[512,2048]{1,0:T(8,128)(2,1)}, u32[]{:S(2)}) copy-start(bf16[512,2048]{1,0:T(8,128)(2,1)} %param.28) | copy-start | bytes 6291460
  7.2 78.8 %all-gather.5.cloned.1.call-start = ((), (), s32[]{:S(2)}) async-start(), calls=%async_computation.4 | async-start | bytes 8912896 | tf_op jit(solution)/shard_map/all_gather | solution.py:132
  9.9 83.5 %copy-start.70 = (f32[128]{0:T(128)}, f32[128]{0:T(128)S(1)}, u32[]{:S(2)}) copy-start(f32[128]{0:T(128)S(1)} %fusion.75) | copy-start | bytes 1540
  12.8 236.2 %reduce-scatter.5.cloned.1.call-start = ((), (), s32[]{:S(2)}) async-start(), calls=%async_computation.5 | async-start | bytes 17825792 | tf_op jit(solution)/shard_map/reduce_scatter | solution.py:166
  16.1 689.9 %copy-start.47 = (s32[512]{0:T(512)}, s32[512]{0:T(512)S(1)}, u32[]{:S(2)}) copy-start(s32[512]{0:T(512)S(1)} %iota_add_fusion.2) | copy-start | bytes 6148
  16.1 689.9 %copy-start.45 = (s32[512]{0:T(512)}, s32[512]{0:T(512)S(1)}, u32[]{:S(2)}) copy-start(s32[512]{0:T(512)S(1)} %iota_add_fusion) | copy-start | bytes 6148
  93.5 22.0 %copy-start.24 = (bf16[2048,1,128]{2,0,1:T(8,128)(2,1)}, bf16[2048,1,128]{2,0,1:T(8,128)(2,1)S(1)}, u32[]{:S(2)}) copy-start(bf16[2048,1,128]{2,0,1:T(8,128)(2,1)S(1)} %fusion.79) | copy-start | bytes 1572868
  106.0 24.4 %copy-start.27 = (bf16[512,128]{1,0:T(8,128)(2,1)}, bf16[512,128]{1,0:T(8,128)(2,1)S(1)}, u32[]{:S(2)}) copy-start(bf16[512,128]{1,0:T(8,128)(2,1)S(1)} %convert_element_type.280) | copy-start | bytes 393220
  115.5 14.9 %copy-start.29 = (bf16[512,128]{1,0:T(8,128)(2,1)}, bf16[512,128]{1,0:T(8,128)(2,1)S(1)}, u32[]{:S(2)}) copy-start(bf16[512,128]{1,0:T(8,128)(2,1)S(1)} %convert_element_type.278) | copy-start | bytes 393220
  125.2 13.4 %copy-start.31 = (bf16[512,128]{1,0:T(8,128)(2,1)}, bf16[512,128]{1,0:T(8,128)(2,1)S(1)}, u32[]{:S(2)}) copy-start(bf16[512,128]{1,0:T(8,128)(2,1)S(1)} %convert_element_type.276) | copy-start | bytes 393220
  138.5 110.5 %copy-start.58 = (f32[2048]{0:T(1024)S(1)}, f32[2048]{0:T(1024)}, u32[]{:S(2)}) copy-start(f32[2048]{0:T(1024)} %param.23) | copy-start | bytes 24580
  138.5 112.3 %copy-start.43 = (f32[2048]{0:T(1024)S(1)}, f32[2048]{0:T(1024)}, u32[]{:S(2)}) copy-start(f32[2048]{0:T(1024)} %param.24) | copy-start | bytes 24580
  138.5 112.3 %copy-start.59 = (f32[2048]{0:T(1024)S(1)}, f32[2048]{0:T(1024)}, u32[]{:S(2)}) copy-start(f32[2048]{0:T(1024)} %param.25) | copy-start | bytes 24580
  138.6 183.7 %all-gather.7.cloned.1.call-start = ((), (), s32[]{:S(2)}) async-start(), calls=%async_computation.6 | async-start | bytes 8912896 | tf_op jit(solution)/shard_map/all_gather | solution.py:176
  251.9 143.3 %all-gather.9.cloned.1.call-start = ((), (), s32[]{:S(2)}) async-start(), calls=%async_computation.8 | async-start | bytes 8912896 | tf_op jit(solution)/shard_map/all_gather | solution.py:202
  254.7 140.5 %copy-start.72 = (f32[512]{0:T(512)S(1)}, f32[512]{0:T(512)}, u32[]{:S(2)}) copy-start(f32[512]{0:T(512)} %param.27) | copy-start | bytes 6148
  254.7 273.3 %reduce-scatter.9.cloned.1.call-start = ((), (), s32[]{:S(2)}) async-start(), calls=%async_computation.9 | async-start | bytes 17825792 | tf_op jit(solution)/shard_map/reduce_scatter | solution.py:218
  395.2 14.1 %copy-start.71 = (bf16[2048,512]{1,0:T(8,128)(2,1)S(1)}, bf16[2048,512]{1,0:T(8,128)(2,1)}, u32[]{:S(2)}) copy-start(bf16[2048,512]{1,0:T(8,128)(2,1)} %param.26) | copy-start | bytes 6291460
  417.6 198.4 %reduce-scatter.7.cloned.1.call-start = ((), (), s32[]{:S(2)}) async-start(), calls=%async_computation.7 | async-start | bytes 8912896 | tf_op jit(solution)/shard_map/reduce_scatter | solution.py:188
  427.9 188.1 %copy-start.60 = (f32[2048]{0:T(1024)S(1)}, f32[2048]{0:T(1024)}, u32[]{:S(2)}) copy-start(f32[2048]{0:T(1024)} %param.29) | copy-start | bytes 24580
  427.9 190.6 %copy-start.21 = (bf16[128,1,2048]{2,0,1:T(8,128)(2,1)S(1)}, bf16[128,1,2048]{2,0,1:T(8,128)(2,1)}, u32[]{:S(2)}) copy-start(bf16[128,1,2048]{2,0,1:T(8,128)(2,1)} %get-tuple-element.79) | copy-start | bytes 1572868
  427.9 261.9 %all-gather.11.cloned.1.call-start = ((), (), s32[]{:S(2)}) async-start(), calls=%async_computation.10 | async-start | bytes 8912896 | tf_op jit(solution)/shard_map/all_gather | solution.py:230
  619.7 252.5 %reduce-scatter.11.cloned.1.call-start = ((), (), s32[]{:S(2)}) async-start(), calls=%async_computation.11 | async-start | bytes 8912896 | tf_op jit(solution)/shard_map/reduce_scatter | solution.py:250
  624.1 81.8 %copy-start.49 = (f32[512]{0:T(512)}, f32[512]{0:T(512)S(1)}, u32[]{:S(2)}) copy-start(f32[512]{0:T(512)S(1)} %get-tuple-element.118) | copy-start | bytes 6148
  624.1 81.8 %copy-start.51 = (f32[512]{0:T(512)}, f32[512]{0:T(512)S(1)}, u32[]{:S(2)}) copy-start(f32[512]{0:T(512)S(1)} %get-tuple-element.117) | copy-start | bytes 6148
  624.6 65.3 %copy-start.38 = (bf16[1,128,2048]{2,1,0:T(8,128)(2,1)S(1)}, bf16[1,128,2048]{2,1,0:T(8,128)(2,1)}, u32[]{:S(2)}) copy-start(bf16[1,128,2048]{2,1,0:T(8,128)(2,1)} %param.22) | copy-start | bytes 1572868
  626.8 79.2 %copy-start.53 = (f32[512]{0:T(512)}, f32[512]{0:T(512)S(1)}, u32[]{:S(2)}) copy-start(f32[512]{0:T(512)S(1)} %get-tuple-element.119) | copy-start | bytes 6148
  626.8 79.2 %copy-start.55 = (f32[512]{0:T(512)}, f32[512]{0:T(512)S(1)}, u32[]{:S(2)}) copy-start(f32[512]{0:T(512)S(1)} %get-tuple-element.120) | copy-start | bytes 6148
  717.9 11.5 %copy-start.25 = (bf16[2048,1,128]{2,0,1:T(8,128)(2,1)S(1)}, bf16[2048,1,128]{2,0,1:T(8,128)(2,1)}, u32[]{:S(2)}) copy-start(bf16[2048,1,128]{2,0,1:T(8,128)(2,1)} %copy-done.24) | copy-start | bytes 1572868
  742.9 11.3 %copy-start.16 = (bf16[2048,1,3,128]{3,0,2,1:T(8,128)(2,1)}, bf16[2048,1,3,128]{3,0,2,1:T(8,128)(2,1)S(1)}, u32[]{:S(2)}) copy-start(bf16[2048,1,3,128]{3,0,2,1:T(8,128)(2,1)S(1)} %pad_maximum_fusion) | copy-start | bytes 4718596
  776.8 26.3 %collective-permute-start.13 = (bf16[4,256,512]{2,1,0:T(8,128)(2,1)}, bf16[4,256,512]{2,1,0:T(8,128)(2,1)S(1)}, u32[]{:S(2)}, u32[]{:S(2)}) collective-permute-start(bf16[4,256,512]{2,1,0:T(8,128)(2,1)} %bitcast.57), channel_id=1, source_target_pairs={{0,64},{32,96},{64,0},{96,32},{1,65},{33,97},{65,1},{97,33},{2,66}... | collective-permute-start | bytes 3145736 | tf_op jit(solution)/shard_map/ppermute | solution.py:343
  781.9 42.6 %collective-permute-start.16 = (bf16[512,4,256]{2,0,1:T(8,128)(2,1)}, bf16[512,4,256]{2,0,1:T(8,128)(2,1)}, u32[]{:S(2)}, u32[]{:S(2)}) collective-permute-start(bf16[512,4,256]{2,0,1:T(8,128)(2,1)} %select_convert_fusion), channel_id=1, source_target_pairs={{0,64},{32,96},{64,0},{96,32},{1,65},{33,97},{65,1},{97,33},{2,66}... | collective-permute-start | bytes 3145736 | tf_op jit(solution)/shard_map/ppermute | solution.py:343
  786.0 38.4 %copy-start.13 = (f32[512,4,256]{2,1,0:T(4,128)S(1)}, f32[512,4,256]{2,1,0:T(4,128)}, u32[]{:S(2)}) copy-start(f32[512,4,256]{2,1,0:T(4,128)} %copy-done.12) | copy-start | bytes 6291460
  803.5 23.1 %collective-permute-start.14 = (bf16[2,256,512]{2,1,0:T(8,128)(2,1)S(1)}, bf16[2,256,512]{2,1,0:T(8,128)(2,1)S(1)}, u32[]{:S(2)}, u32[]{:S(2)}) collective-permute-start(bf16[2,256,512]{2,1,0:T(8,128)(2,1)S(1)} %select_convert_fusion.4), channel_id=1, source_target_pairs={{0,32},{32,0},{64,96},{96,64},{1,33},{33,1},{65,97},{97,65},{2,34}... | collective-permute-start | bytes 1572872 | tf_op jit(solution)/shard_map/ppermute | solution.py:343
  826.5 3.7 collective-permute-start.17
  827.0 16.8 %copy-start.44 = (f32[2048]{0:T(1024)S(1)}, f32[2048]{0:T(1024)}, u32[]{:S(2)}) copy-start(f32[2048]{0:T(1024)} %get-tuple-element.55) | copy-start | bytes 24580
  827.0 19.7 %copy-start.28 = (bf16[512,128]{1,0:T(8,128)(2,1)S(1)}, bf16[512,128]{1,0:T(8,128)(2,1)}, u32[]{:S(2)}) copy-start(bf16[512,128]{1,0:T(8,128)(2,1)} %copy-done.27) | copy-start | bytes 393220
  827.0 19.7 %copy-start.30 = (bf16[512,128]{1,0:T(8,128)(2,1)S(1)}, bf16[512,128]{1,0:T(8,128)(2,1)}, u32[]{:S(2)}) copy-start(bf16[512,128]{1,0:T(8,128)(2,1)} %copy-done.29) | copy-start | bytes 393220
  827.0 19.7 %copy-start.32 = (bf16[512,128]{1,0:T(8,128)(2,1)S(1)}, bf16[512,128]{1,0:T(8,128)(2,1)}, u32[]{:S(2)}) copy-start(bf16[512,128]{1,0:T(8,128)(2,1)} %copy-done.31) | copy-start | bytes 393220
  827.0 19.6 %copy-start.34 = (bf16[512,128]{1,0:T(8,128)(2,1)S(1)}, bf16[512,128]{1,0:T(8,128)(2,1)}, u32[]{:S(2)}) copy-start(bf16[512,128]{1,0:T(8,128)(2,1)} %copy-done.33) | copy-start | bytes 393220
  827.0 10.7 %collective-permute-start.15 = (bf16[1,256,512]{2,1,0:T(8,128)(2,1)S(1)}, bf16[1,256,512]{2,1,0:T(8,128)(2,1)S(1)}, u32[]{:S(2)}, u32[]{:S(2)}) collective-permute-start(bf16[1,256,512]{2,1,0:T(8,128)(2,1)S(1)} %select_convert_fusion.6), channel_id=1, source_target_pairs={{0,16},{16,0},{1,17},{17,1},{2,18},{18,2},{3,19},{19,3},{4,20},{20... | collective-permute-start | bytes 786440 | tf_op jit(solution)/shard_map/ppermute | solution.py:343
  831.2 11.7 %collective-permute-start.18 = (bf16[512,1,256]{2,0,1:T(8,128)(2,1)}, bf16[512,1,256]{2,0,1:T(8,128)(2,1)S(1)}, u32[]{:S(2)}, u32[]{:S(2)}) collective-permute-start(bf16[512,1,256]{2,0,1:T(8,128)(2,1)} %select_convert_fusion.5), channel_id=1, source_target_pairs={{0,16},{16,0},{1,17},{17,1},{2,18},{18,2},{3,19},{19,3},{4,20},{20... | collective-permute-start | bytes 786440 | tf_op jit(solution)/shard_map/ppermute | solution.py:343
  852.0 10.2 %collective-permute-start.10 = (bf16[1,128,4,256]{3,1,2,0:T(8,128)(2,1)S(1)}, bf16[1,128,4,256]{3,1,2,0:T(8,128)(2,1)S(1)}, u32[]{:S(2)}, u32[]{:S(2)}) collective-permute-start(bf16[1,128,4,256]{3,1,2,0:T(8,128)(2,1)S(1)} %select_convert_fusion.7), channel_id=1, source_target_pairs={{0,64},{32,96},{64,0},{96,32},{1,65},{33,97},{65,1},{97,33},{2,66}... | collective-permute-start | bytes 786440 | tf_op jit(solution)/shard_map/ppermute | solution.py:343
  862.2 12.1 %copy-start.63 = (f32[128]{0:T(128)S(1)}, f32[128]{0:T(128)}, u32[]{:S(2)}) copy-start(f32[128]{0:T(128)} %copy-done.62) | copy-start | bytes 1540
  862.4 13.7 %copy-start.39 = (f32[8,16,16]{2,1,0:T(8,128)S(1)}, f32[8,16,16]{2,1,0:T(8,128)}, u32[]{:S(2)}) copy-start(f32[8,16,16]{2,1,0:T(8,128)} %mul.436) | copy-start | bytes 24580
  862.4 13.7 %copy-start.40 = (f32[8,16,16]{2,1,0:T(8,128)S(1)}, f32[8,16,16]{2,1,0:T(8,128)}, u32[]{:S(2)}) copy-start(f32[8,16,16]{2,1,0:T(8,128)} %mul.434) | copy-start | bytes 24580
  862.4 13.7 %copy-start.41 = (f32[8,16,16]{2,1,0:T(8,128)S(1)}, f32[8,16,16]{2,1,0:T(8,128)}, u32[]{:S(2)}) copy-start(f32[8,16,16]{2,1,0:T(8,128)} %mul.431) | copy-start | bytes 24580
  862.4 1.4 collective-permute-start.11
  864.6 6.1 collective-permute-start.12
  869.5 36.4 %collective-permute-start.7 = (bf16[4,256,3,1,128]{4,3,2,1,0:T(2,128)(2,1)S(1)}, bf16[4,256,3,1,128]{4,3,2,1,0:T(2,128)(2,1)}, u32[]{:S(2)}, u32[]{:S(2)}) collective-permute-start(bf16[4,256,3,1,128]{4,3,2,1,0:T(2,128)(2,1)S(1)} %copy.55), channel_id=1, source_target_pairs={{0,64},{32,96},{64,0},{96,32},{1,65},{33,97},{65,1},{97,33},{2,66}... | collective-permute-start | bytes 2359304 | tf_op jit(solution)/shard_map/ppermute | solution.py:343
  877.2 33.0 %collective-permute-start = (f32[8,8,192]{2,0,1:T(8,128)S(1)}, f32[8,8,192]{2,0,1:T(8,128)S(1)}, u32[]{:S(2)}, u32[]{:S(2)}) collective-permute-start(f32[8,8,192]{2,0,1:T(8,128)S(1)} %slice_select_fusion.2), channel_id=1, source_target_pairs={{0,8},{1,9},{2,10},{3,11},{4,12},{5,13},{6,14},{7,15},{8,0},{9,1},... | collective-permute-start | bytes 147464 | tf_op jit(solution)/shard_map/ppermute | solution.py:343
  910.2 24.2 %copy-start.20 = (f32[128,1,2048]{2,0,1:T(8,128)S(1)}, f32[128,1,2048]{2,0,1:T(8,128)}, u32[]{:S(2)}) copy-start(f32[128,1,2048]{2,0,1:T(8,128)} %copy-done.19) | copy-start | bytes 3145732
  910.2 24.2 %copy-start.22 = (bf16[128,1,2048]{2,0,1:T(8,128)(2,1)S(1)}, bf16[128,1,2048]{2,0,1:T(8,128)(2,1)}, u32[]{:S(2)}) copy-start(bf16[128,1,2048]{2,0,1:T(8,128)(2,1)} %get-tuple-element.79) | copy-start | bytes 1572868
  910.2 24.2 %copy-start.23 = (bf16[128,1,2048]{2,0,1:T(8,128)(2,1)S(1)}, bf16[128,1,2048]{2,0,1:T(8,128)(2,1)}, u32[]{:S(2)}) copy-start(bf16[128,1,2048]{2,0,1:T(8,128)(2,1)} %reduce-scatter.11.cloned.1.call-done) | copy-start | bytes 1572868
  910.2 24.2 %copy-start.65 = (f32[128]{0:T(128)S(1)}, f32[128]{0:T(128)}, u32[]{:S(2)}) copy-start(f32[128]{0:T(128)} %copy-done.64) | copy-start | bytes 1540
  910.2 4.0 collective-permute-start.1
  912.5 4.8 collective-permute-start.8
  914.2 26.2 %copy-start.1 = (bf16[512,2048]{1,0:T(8,128)(2,1)S(1)}, bf16[512,2048]{1,0:T(8,128)(2,1)}, u32[]{:S(2)}) copy-start(bf16[512,2048]{1,0:T(8,128)(2,1)} %param.28) | copy-start | bytes 6291460
  914.3 5.3 collective-permute-start.2
  919.6 3.7 collective-permute-start.3
  921.5 9.4 collective-permute-start.9
  923.4 8.9 collective-permute-start.4
  932.4 1.2 collective-permute-start.5
  933.6 5.2 collective-permute-start.6
  (40 other events, 168.1 us)
Sparse Core Ops, SparseCore 0:
  12.9 73.0 all-gather.4
  138.7 110.2 reduce-scatter.4
  252.1 70.1 all-gather.6
  324.8 70.3 all-gather.8
  417.7 110.1 reduce-scatter.8
  531.2 84.7 reduce-scatter.6
  619.8 70.0 all-gather.10
  754.4 84.8 reduce-scatter.10
where the time goes:
time: 957 us; the launch traced here: 948 us
  waiting for transfers between devices  645 us (67%)
  matrix products  149 us (16%)
  other arithmetic  72.5 us (8%)
  starting transfers between devices  24.1 us (3%)
  local copies, waits for them, and re-layouts  24 us (3%)
  between operations  17.3 us (2%)
  Pallas kernels  16.2 us (2%)
    reduce_scatter x1, waiting for transfers between devices, shards(): lax.psum_scatter(jnp.einsum('rse,ed->rsd', piece, out_weight, preferred_e...  110 us
    reduce_scatter x1, waiting for transfers between devices, shards(): lax.psum_scatter(jnp.einsum('rsf,df->rsd', piece, w_in, preferred_element...  100 us
    ppermute x19, waiting for transfers between devices, halving_steps(): got = lax.ppermute(send, axis, [(i, i ^ bit) for i in range(size)])  87.8 us
    reduce_scatter x1, waiting for transfers between devices, shards(): lax.psum_scatter(jnp.einsum('rsf,fd->rsd', piece, w_out, preferred_elemen...  85.8 us
    all_gather x1, waiting for transfers between devices, shards(): normed_full = lax.all_gather(normed_low, 'tensor', axis=0, tiled=True)  69.2 us
    all_gather x1, waiting for transfers between devices, shards(): second_full = lax.all_gather(second_low, 'tensor', axis=0, tiled=True)  67.5 us
    all_gather x1, waiting for transfers between devices, shards(): piece = lax.all_gather(upstream, 'tensor', axis=0, tiled=True)  62.4 us
    all_gather x1, waiting for transfers between devices, shards(): piece = lax.all_gather(branch_low, 'tensor', axis=0, tiled=True)  61.8 us
  transfers between devices with their start and end apart: 27, of which 20 were waited for; matrix products, arithmetic and copies ran while one was open for 11% of the time, Pallas kernels for 0%

commit v1 on v0

--- a/solution.py
+++ b/solution.py
@@ -7,6 +7,13 @@
 
 EPS = 1e-05
 NEGATIVE = -1e30
+
+
+def all_by_exchange(value, name, along):
+    peers = lax.axis_size(name)
+    parts = jnp.stack([value for _ in range(peers)])
+    parts = lax.all_to_all(parts, name, split_axis=0, concat_axis=0)
+    return jnp.concatenate(parts, axis=along)
 
 
 def layer_norm(value, gain, shift):
@@ -129,7 +136,7 @@
     )
     inputs = tokens.astype(jnp.float32)
     normed_low = layer_norm(inputs, ln1_gain, ln1_bias).astype(jnp.bfloat16)
-    normed_full = lax.all_gather(normed_low, "tensor", axis=0, tiled=True)
+    normed_full = all_by_exchange(normed_low, "tensor", 0)
     joint_weight = w_qkv.reshape(model_width, 3 * local_width)
     projected = jnp.dot(
         normed_full.reshape(seq_total * seq_count, model_width),

time: 957 us -> 1050 us (1.097)
  waiting for transfers between devices: 645 us -> 723 us
    all_to_all x0 -> x1, waiting for transfers between devices: none -> 144 us  [all_by_exchange(): parts = lax.all_to_all(parts, name, split_axis=0, concat_axis=0)]
    all_gather x1 -> x0, waiting for transfers between devices: 69.2 us -> none  [shards(): normed_full = lax.all_gather(normed_low, 'tensor', axis=0, tiled=True)]
  transfers between devices with their start and end apart: 27 -> 27, of which waited for: 20 -> 20; matrix products, arithmetic and copies ran while one was open for 11% -> 10% of each run, Pallas kernels for 0% -> 0%
where the time goes in v1:
time: 1050 us; the launch traced here: 1040 us
  waiting for transfers between devices  723 us (69%)
  matrix products  149 us (14%)
  other arithmetic  71.7 us (7%)
  starting transfers between devices  31.5 us (3%)
  local copies, waits for them, and re-layouts  28.8 us (3%)
  between operations  17.2 us (2%)
  Pallas kernels  16.2 us (2%)
    all_to_all x1, waiting for transfers between devices, all_by_exchange(): parts = lax.all_to_all(parts, name, split_axis=0, concat_axis=0)  144 us
    reduce_scatter x1, waiting for transfers between devices, shards(): lax.psum_scatter(jnp.einsum('rse,ed->rsd', piece, out_weight, preferred_e...  114 us
    reduce_scatter x1, waiting for transfers between devices, shards(): lax.psum_scatter(jnp.einsum('rsf,df->rsd', piece, w_in, preferred_element...  100 us
    ppermute x19, waiting for transfers between devices, halving_steps(): got = lax.ppermute(send, axis, [(i, i ^ bit) for i in range(size)])  87.7 us
    reduce_scatter x1, waiting for transfers between devices, shards(): lax.psum_scatter(jnp.einsum('rsf,fd->rsd', piece, w_out, preferred_elemen...  85.6 us
    all_gather x1, waiting for transfers between devices, shards(): second_full = lax.all_gather(second_low, 'tensor', axis=0, tiled=True)  67.6 us
    all_gather x1, waiting for transfers between devices, shards(): piece = lax.all_gather(upstream, 'tensor', axis=0, tiled=True)  62.5 us
    all_gather x1, waiting for transfers between devices, shards(): piece = lax.all_gather(branch_low, 'tensor', axis=0, tiled=True)  61.8 us
  transfers between devices with their start and end apart: 27, of which 20 were waited for; matrix products, arithmetic and copies ran while one was open for 10% of the time, Pallas kernels for 0%

profile of v1, /device:TPU:0, one launch (start us, length us, event | category | flops | bytes accessed | tf_op | source)
XLA Modules:
  0.0 1037.3 jit_solution(14607841363049635191)
XLA Ops:
  12.4 4.3 stack.10
  16.7 7.3 all-to-all-start
  24.1 2.6 copy.61
  28.0 143.7 %all-to-all-done = bf16[16,128,1,2048]{3,1,2,0:T(8,128)(2,1)} async-done(((bf16[16,128,1,2048]{3,1,2,0:T(8,128)(2,1)}), bf16[16,128,1,2048]{3,1,2,0:T(8,128)(2,1)}, u32[]{:S(2)}, u32[]{:S(2)}) %all-to-all-start) | async-done | bytes 8388640 | tf_op jit(solution)/shard_map/all_to_all | solution.py:15
  171.7 7.4 convolution_bitcast_fusion.2
  180.4 2.9 fusion.110
  183.4 3.3 fusion.113
  186.7 4.0 online-softmax.3
  191.7 4.6 fusion.112
  196.3 4.0 online-softmax.2
  201.2 4.6 fusion.111
  205.9 4.0 online-softmax.1
  210.9 4.2 online-softmax
  216.1 8.1 convolution_bitcast_fusion.1
  224.3 114.3 %reduce-scatter.5.cloned.1.call-done = f32[128,1,2048]{2,0,1:T(8,128)} async-done(((f32[2048,1,2048]{2,0,1:T(8,128)}), f32[128,1,2048]{2,0,1:T(8,128)}) %reduce-scatter.5.cloned.1.call-update) | async-done | bytes 1048592 | tf_op jit(solution)/shard_map/reduce_scatter | solution.py:173
  342.3 2.0 convert_reduce_fusion.4
  344.4 67.6 %all-gather.4.cloned.1.call-done = bf16[2048,1,2048]{2,0,1:T(8,128)(2,1)} async-done(((bf16[128,1,2048]{2,0,1:T(8,128)(2,1)}), bf16[2048,1,2048]{2,0,1:T(8,128)(2,1)}) %all-gather.4.cloned.1.call-update) | async-done | bytes 8388624 | tf_op jit(solution)/shard_map/all_gather | solution.py:183
  411.9 10.6 %fusion.10 = f32[2048,512]{1,0:T(8,128)} fusion(bf16[2048,512]{1,0:T(8,128)(2,1)} %param.26, bf16[2048,1,2048]{2,0,1:T(8,128)(2,1)} %all-gather.4.cloned.1.call-done), kind=kOutput, calls=%fused_computation.12 | convolution fusion | flops 4294967296 | bytes 14680064 | tf_op jit(solution)/shard_map/dot_general | solution.py:185
  422.5 62.5 %all-gather.6.cloned.1.call-done = bf16[2048,1,2048]{2,0,1:T(8,128)(2,1)} async-done(((bf16[128,1,2048]{2,0,1:T(8,128)(2,1)}), bf16[2048,1,2048]{2,0,1:T(8,128)(2,1)}) %all-gather.6.cloned.1.call-update) | async-done | bytes 8388624 | tf_op jit(solution)/shard_map/all_gather | solution.py:209
  485.0 12.7 %convert_reduce_fusion = (f32[512]{0:T(512)}, bf16[2048,512]{1,0:T(8,128)(2,1)S(1)}) fusion(f32[2048,512]{1,0:T(8,128)} %fusion.10, f32[512]{0:T(512)S(1)} %copy-done.72, bf16[512,2048]{1,0:T(8,128)(2,1)S(1)} %copy-done, bf16[2048,1,2048]{2,0,1:T(8,128)(2,1)} %all-gather.6.cloned.1.call-done), kind=kOutput, calls=%fused_computation.25 | convolution fusion | flops 4319084032 | bytes 16781312 | tf_op jit(solution)/shard_map/rsd,fd->rsf/dot_general | solution.py:211
  499.1 8.2 convolution_bitcast_fusion
  507.3 10.2 convert_bitcast_fusion.1
  517.7 100.0 %reduce-scatter.9.cloned.1.call-done = f32[128,1,2048]{2,0,1:T(8,128)} async-done(((f32[2048,1,2048]{2,0,1:T(8,128)}), f32[128,1,2048]{2,0,1:T(8,128)}) %reduce-scatter.9.cloned.1.call-update) | async-done | bytes 1048592 | tf_op jit(solution)/shard_map/reduce_scatter | solution.py:225
  617.7 2.2 multiply_reduce_fusion.4
  620.0 85.6 %reduce-scatter.7.cloned.1.call-done = bf16[128,1,2048]{2,0,1:T(8,128)(2,1)} async-done(((bf16[2048,1,2048]{2,0,1:T(8,128)(2,1)}), bf16[128,1,2048]{2,0,1:T(8,128)(2,1)}) %reduce-scatter.7.cloned.1.call-update) | async-done | bytes 524304 | tf_op jit(solution)/shard_map/reduce_scatter | solution.py:195
  705.6 2.6 fusion.106
  709.5 3.0 exponential_reduce_fusion
  717.7 61.8 %all-gather.8.cloned.1.call-done = bf16[2048,1,2048]{2,0,1:T(8,128)(2,1)} async-done(((bf16[128,1,2048]{2,0,1:T(8,128)(2,1)}), bf16[2048,1,2048]{2,0,1:T(8,128)(2,1)}) %all-gather.8.cloned.1.call-update) | async-done | bytes 8388624 | tf_op jit(solution)/shard_map/all_gather | solution.py:237
  779.4 5.7 fusion.35
  785.2 2.7 fusion.87
  787.9 2.8 fusion.90
  790.7 2.8 fusion.93
  793.6 1.9 fusion.45
  797.2 10.2 multiply_reduce_fusion
  807.4 9.4 multiply_convert_fusion
  816.9 2.0 fusion.62
  819.8 1.7 convolution_add_fusion.2
  821.5 1.7 convolution_add_fusion.1
  823.2 2.0 fusion.40
  825.4 2.4 multiply_convert_fusion.1
  832.4 1.6 copy.70
  834.1 9.7 convert_bitcast_fusion
  847.2 8.7 fusion.23
  855.9 2.0 copy.93
  857.9 7.1 fusion.26
  872.8 2.8 slice_select_fusion
  875.6 17.0 %collective-permute-done.13 = bf16[4,256,512]{2,1,0:T(8,128)(2,1)S(1)} collective-permute-done((bf16[4,256,512]{2,1,0:T(8,128)(2,1)}, bf16[4,256,512]{2,1,0:T(8,128)(2,1)S(1)}, u32[]{:S(2)}, u32[]{:S(2)}) %collective-permute-start.13) | collective-permute-done | bytes 1048608 | tf_op jit(solution)/shard_map/ppermute | solution.py:350
  893.1 20.9 %collective-permute-done.16 = bf16[512,4,256]{2,0,1:T(8,128)(2,1)} collective-permute-done((bf16[512,4,256]{2,0,1:T(8,128)(2,1)}, bf16[512,4,256]{2,0,1:T(8,128)(2,1)}, u32[]{:S(2)}, u32[]{:S(2)}) %collective-permute-start.16) | collective-permute-done | bytes 1048608 | tf_op jit(solution)/shard_map/ppermute | solution.py:350
  914.0 2.0 convert_add_fusion
  916.5 3.2 collective-permute-start.15
  920.8 1.6 collective-permute-start.18
  923.8 3.4 collective-permute-done.15
  928.2 4.3 collective-permute-done.18
  936.2 4.7 fusion.32
  941.5 1.6 collective-permute-start.10
  943.2 7.0 convolution_multiply_fusion
  954.1 2.9 collective-permute-start.12
  966.7 3.3 collective-permute-start
  970.0 25.4 %collective-permute-done.7 = bf16[4,256,3,1,128]{4,3,2,1,0:T(2,128)(2,1)} collective-permute-done((bf16[4,256,3,1,128]{4,3,2,1,0:T(2,128)(2,1)S(1)}, bf16[4,256,3,1,128]{4,3,2,1,0:T(2,128)(2,1)}, u32[]{:S(2)}, u32[]{:S(2)}) %collective-permute-start.7) | collective-permute-done | bytes 786464 | tf_op jit(solution)/shard_map/ppermute | solution.py:350
  995.4 4.3 copy_add_fusion
  1002.2 1.6 collective-permute-done.1
  1003.8 3.1 collective-permute-start.2
  1013.3 7.1 collective-permute-done.9
  1025.3 3.0 collective-permute-done.6
  (309 shorter events, 78.1 us)
Async XLA Ops:
  7.2 477.8 %copy-start = (bf16[512,2048]{1,0:T(8,128)(2,1)S(1)}, bf16[512,2048]{1,0:T(8,128)(2,1)}, u32[]{:S(2)}) copy-start(bf16[512,2048]{1,0:T(8,128)(2,1)} %param.28) | copy-start | bytes 6291460
  16.7 11.3 %copy-start.67 = (f32[2,128]{1,0:T(2,128)S(1)}, f32[2,128]{1,0:T(2,128)}, u32[]{:S(2)}) copy-start(f32[2,128]{1,0:T(2,128)} %param.21) | copy-start | bytes 3076
  16.7 155.0 %all-to-all-start = ((bf16[16,128,1,2048]{3,1,2,0:T(8,128)(2,1)}), bf16[16,128,1,2048]{3,1,2,0:T(8,128)(2,1)}, u32[]{:S(2)}, u32[]{:S(2)}) async-start(bf16[16,128,1,2048]{3,1,2,0:T(8,128)(2,1)} %stack.10), calls=%async_computation | async-start | bytes 16777216 | tf_op jit(solution)/shard_map/all_to_all | solution.py:15
  24.0 314.5 %reduce-scatter.5.cloned.1.call-start = ((), (), s32[]{:S(2)}) async-start(), calls=%async_computation.5 | async-start | bytes 17825792 | tf_op jit(solution)/shard_map/reduce_scatter | solution.py:173
  27.3 768.1 %copy-start.47 = (s32[512]{0:T(512)}, s32[512]{0:T(512)S(1)}, u32[]{:S(2)}) copy-start(s32[512]{0:T(512)S(1)} %iota_add_fusion.2) | copy-start | bytes 6148
  27.3 768.1 %copy-start.45 = (s32[512]{0:T(512)}, s32[512]{0:T(512)S(1)}, u32[]{:S(2)}) copy-start(s32[512]{0:T(512)S(1)} %iota_add_fusion) | copy-start | bytes 6148
  179.2 22.0 %copy-start.24 = (bf16[2048,1,128]{2,0,1:T(8,128)(2,1)}, bf16[2048,1,128]{2,0,1:T(8,128)(2,1)S(1)}, u32[]{:S(2)}) copy-start(bf16[2048,1,128]{2,0,1:T(8,128)(2,1)S(1)} %fusion.69) | copy-start | bytes 1572868
  191.7 24.4 %copy-start.27 = (bf16[512,128]{1,0:T(8,128)(2,1)}, bf16[512,128]{1,0:T(8,128)(2,1)S(1)}, u32[]{:S(2)}) copy-start(bf16[512,128]{1,0:T(8,128)(2,1)S(1)} %convert_element_type.283) | copy-start | bytes 393220
  201.2 14.9 %copy-start.29 = (bf16[512,128]{1,0:T(8,128)(2,1)}, bf16[512,128]{1,0:T(8,128)(2,1)S(1)}, u32[]{:S(2)}) copy-start(bf16[512,128]{1,0:T(8,128)(2,1)S(1)} %convert_element_type.281) | copy-start | bytes 393220
  210.9 13.3 %copy-start.31 = (bf16[512,128]{1,0:T(8,128)(2,1)}, bf16[512,128]{1,0:T(8,128)(2,1)S(1)}, u32[]{:S(2)}) copy-start(bf16[512,128]{1,0:T(8,128)(2,1)S(1)} %convert_element_type.279) | copy-start | bytes 393220
  224.2 114.4 %copy-start.58 = (f32[2048]{0:T(1024)S(1)}, f32[2048]{0:T(1024)}, u32[]{:S(2)}) copy-start(f32[2048]{0:T(1024)} %param.23) | copy-start | bytes 24580
  224.2 116.2 %copy-start.43 = (f32[2048]{0:T(1024)S(1)}, f32[2048]{0:T(1024)}, u32[]{:S(2)}) copy-start(f32[2048]{0:T(1024)} %param.24) | copy-start | bytes 24580
  224.2 116.2 %copy-start.59 = (f32[2048]{0:T(1024)S(1)}, f32[2048]{0:T(1024)}, u32[]{:S(2)}) copy-start(f32[2048]{0:T(1024)} %param.25) | copy-start | bytes 24580
  224.3 187.7 %all-gather.4.cloned.1.call-start = ((), (), s32[]{:S(2)}) async-start(), calls=%async_computation.6 | async-start | bytes 8912896 | tf_op jit(solution)/shard_map/all_gather | solution.py:183
  341.5 143.5 %all-gather.6.cloned.1.call-start = ((), (), s32[]{:S(2)}) async-start(), calls=%async_computation.8 | async-start | bytes 8912896 | tf_op jit(solution)/shard_map/all_gather | solution.py:209
  344.3 140.7 %copy-start.72 = (f32[512]{0:T(512)S(1)}, f32[512]{0:T(512)}, u32[]{:S(2)}) copy-start(f32[512]{0:T(512)} %param.27) | copy-start | bytes 6148
  344.3 273.4 %reduce-scatter.9.cloned.1.call-start = ((), (), s32[]{:S(2)}) async-start(), calls=%async_computation.9 | async-start | bytes 17825792 | tf_op jit(solution)/shard_map/reduce_scatter | solution.py:225
  485.0 14.0 %copy-start.71 = (bf16[2048,512]{1,0:T(8,128)(2,1)S(1)}, bf16[2048,512]{1,0:T(8,128)(2,1)}, u32[]{:S(2)}) copy-start(bf16[2048,512]{1,0:T(8,128)(2,1)} %param.26) | copy-start | bytes 6291460
  507.3 198.3 %reduce-scatter.7.cloned.1.call-start = ((), (), s32[]{:S(2)}) async-start(), calls=%async_computation.7 | async-start | bytes 8912896 | tf_op jit(solution)/shard_map/reduce_scatter | solution.py:195
  517.6 188.0 %copy-start.60 = (f32[2048]{0:T(1024)S(1)}, f32[2048]{0:T(1024)}, u32[]{:S(2)}) copy-start(f32[2048]{0:T(1024)} %param.29) | copy-start | bytes 24580
  517.6 190.5 %copy-start.21 = (bf16[128,1,2048]{2,0,1:T(8,128)(2,1)S(1)}, bf16[128,1,2048]{2,0,1:T(8,128)(2,1)}, u32[]{:S(2)}) copy-start(bf16[128,1,2048]{2,0,1:T(8,128)(2,1)} %get-tuple-element.79) | copy-start | bytes 1572868
  517.6 261.8 %all-gather.8.cloned.1.call-start = ((), (), s32[]{:S(2)}) async-start(), calls=%async_computation.10 | async-start | bytes 8912896 | tf_op jit(solution)/shard_map/all_gather | solution.py:237
  709.3 252.4 %reduce-scatter.11.cloned.1.call-start = ((), (), s32[]{:S(2)}) async-start(), calls=%async_computation.11 | async-start | bytes 8912896 | tf_op jit(solution)/shard_map/reduce_scatter | solution.py:257
  713.7 81.8 %copy-start.49 = (f32[512]{0:T(512)}, f32[512]{0:T(512)S(1)}, u32[]{:S(2)}) copy-start(f32[512]{0:T(512)S(1)} %get-tuple-element.118) | copy-start | bytes 6148
  713.7 81.8 %copy-start.51 = (f32[512]{0:T(512)}, f32[512]{0:T(512)S(1)}, u32[]{:S(2)}) copy-start(f32[512]{0:T(512)S(1)} %get-tuple-element.117) | copy-start | bytes 6148
  714.2 65.2 %copy-start.38 = (bf16[1,128,2048]{2,1,0:T(8,128)(2,1)S(1)}, bf16[1,128,2048]{2,1,0:T(8,128)(2,1)}, u32[]{:S(2)}) copy-start(bf16[1,128,2048]{2,1,0:T(8,128)(2,1)} %param.22) | copy-start | bytes 1572868
  716.4 79.1 %copy-start.53 = (f32[512]{0:T(512)}, f32[512]{0:T(512)S(1)}, u32[]{:S(2)}) copy-start(f32[512]{0:T(512)S(1)} %get-tuple-element.119) | copy-start | bytes 6148
  716.4 79.1 %copy-start.55 = (f32[512]{0:T(512)}, f32[512]{0:T(512)S(1)}, u32[]{:S(2)}) copy-start(f32[512]{0:T(512)S(1)} %get-tuple-element.120) | copy-start | bytes 6148
  807.4 11.5 %copy-start.25 = (bf16[2048,1,128]{2,0,1:T(8,128)(2,1)S(1)}, bf16[2048,1,128]{2,0,1:T(8,128)(2,1)}, u32[]{:S(2)}) copy-start(bf16[2048,1,128]{2,0,1:T(8,128)(2,1)} %copy-done.24) | copy-start | bytes 1572868
  832.4 11.3 %copy-start.16 = (bf16[2048,1,3,128]{3,0,2,1:T(8,128)(2,1)}, bf16[2048,1,3,128]{3,0,2,1:T(8,128)(2,1)S(1)}, u32[]{:S(2)}) copy-start(bf16[2048,1,3,128]{3,0,2,1:T(8,128)(2,1)S(1)} %pad_maximum_fusion) | copy-start | bytes 4718596
  866.3 26.3 %collective-permute-start.13 = (bf16[4,256,512]{2,1,0:T(8,128)(2,1)}, bf16[4,256,512]{2,1,0:T(8,128)(2,1)S(1)}, u32[]{:S(2)}, u32[]{:S(2)}) collective-permute-start(bf16[4,256,512]{2,1,0:T(8,128)(2,1)} %bitcast.58), channel_id=1, source_target_pairs={{0,64},{32,96},{64,0},{96,32},{1,65},{33,97},{65,1},{97,33},{2,66}... | collective-permute-start | bytes 3145736 | tf_op jit(solution)/shard_map/ppermute | solution.py:350
  871.4 42.6 %collective-permute-start.16 = (bf16[512,4,256]{2,0,1:T(8,128)(2,1)}, bf16[512,4,256]{2,0,1:T(8,128)(2,1)}, u32[]{:S(2)}, u32[]{:S(2)}) collective-permute-start(bf16[512,4,256]{2,0,1:T(8,128)(2,1)} %select_convert_fusion), channel_id=1, source_target_pairs={{0,64},{32,96},{64,0},{96,32},{1,65},{33,97},{65,1},{97,33},{2,66}... | collective-permute-start | bytes 3145736 | tf_op jit(solution)/shard_map/ppermute | solution.py:350
  875.6 38.4 %copy-start.13 = (f32[512,4,256]{2,1,0:T(4,128)S(1)}, f32[512,4,256]{2,1,0:T(4,128)}, u32[]{:S(2)}) copy-start(f32[512,4,256]{2,1,0:T(4,128)} %copy-done.12) | copy-start | bytes 6291460
  893.0 23.1 %collective-permute-start.14 = (bf16[2,256,512]{2,1,0:T(8,128)(2,1)S(1)}, bf16[2,256,512]{2,1,0:T(8,128)(2,1)S(1)}, u32[]{:S(2)}, u32[]{:S(2)}) collective-permute-start(bf16[2,256,512]{2,1,0:T(8,128)(2,1)S(1)} %select_convert_fusion.4), channel_id=1, source_target_pairs={{0,32},{32,0},{64,96},{96,64},{1,33},{33,1},{65,97},{97,65},{2,34}... | collective-permute-start | bytes 1572872 | tf_op jit(solution)/shard_map/ppermute | solution.py:350
  916.1 3.7 collective-permute-start.17
  916.5 16.8 %copy-start.44 = (f32[2048]{0:T(1024)S(1)}, f32[2048]{0:T(1024)}, u32[]{:S(2)}) copy-start(f32[2048]{0:T(1024)} %get-tuple-element.55) | copy-start | bytes 24580
  916.5 19.7 %copy-start.28 = (bf16[512,128]{1,0:T(8,128)(2,1)S(1)}, bf16[512,128]{1,0:T(8,128)(2,1)}, u32[]{:S(2)}) copy-start(bf16[512,128]{1,0:T(8,128)(2,1)} %copy-done.27) | copy-start | bytes 393220
  916.5 19.7 %copy-start.30 = (bf16[512,128]{1,0:T(8,128)(2,1)S(1)}, bf16[512,128]{1,0:T(8,128)(2,1)}, u32[]{:S(2)}) copy-start(bf16[512,128]{1,0:T(8,128)(2,1)} %copy-done.29) | copy-start | bytes 393220
  916.5 19.6 %copy-start.32 = (bf16[512,128]{1,0:T(8,128)(2,1)S(1)}, bf16[512,128]{1,0:T(8,128)(2,1)}, u32[]{:S(2)}) copy-start(bf16[512,128]{1,0:T(8,128)(2,1)} %copy-done.31) | copy-start | bytes 393220
  916.5 19.6 %copy-start.34 = (bf16[512,128]{1,0:T(8,128)(2,1)S(1)}, bf16[512,128]{1,0:T(8,128)(2,1)}, u32[]{:S(2)}) copy-start(bf16[512,128]{1,0:T(8,128)(2,1)} %copy-done.33) | copy-start | bytes 393220
  916.5 10.7 %collective-permute-start.15 = (bf16[1,256,512]{2,1,0:T(8,128)(2,1)S(1)}, bf16[1,256,512]{2,1,0:T(8,128)(2,1)S(1)}, u32[]{:S(2)}, u32[]{:S(2)}) collective-permute-start(bf16[1,256,512]{2,1,0:T(8,128)(2,1)S(1)} %select_convert_fusion.6), channel_id=1, source_target_pairs={{0,16},{16,0},{1,17},{17,1},{2,18},{18,2},{3,19},{19,3},{4,20},{20... | collective-permute-start | bytes 786440 | tf_op jit(solution)/shard_map/ppermute | solution.py:350
  920.8 11.7 %collective-permute-start.18 = (bf16[512,1,256]{2,0,1:T(8,128)(2,1)}, bf16[512,1,256]{2,0,1:T(8,128)(2,1)S(1)}, u32[]{:S(2)}, u32[]{:S(2)}) collective-permute-start(bf16[512,1,256]{2,0,1:T(8,128)(2,1)} %select_convert_fusion.5), channel_id=1, source_target_pairs={{0,16},{16,0},{1,17},{17,1},{2,18},{18,2},{3,19},{19,3},{4,20},{20... | collective-permute-start | bytes 786440 | tf_op jit(solution)/shard_map/ppermute | solution.py:350
  941.5 10.1 collective-permute-start.10
  951.7 12.1 %copy-start.63 = (f32[128]{0:T(128)S(1)}, f32[128]{0:T(128)}, u32[]{:S(2)}) copy-start(f32[128]{0:T(128)} %copy-done.62) | copy-start | bytes 1540
  951.9 13.7 %copy-start.39 = (f32[8,16,16]{2,1,0:T(8,128)S(1)}, f32[8,16,16]{2,1,0:T(8,128)}, u32[]{:S(2)}) copy-start(f32[8,16,16]{2,1,0:T(8,128)} %mul.436) | copy-start | bytes 24580
  951.9 13.7 %copy-start.40 = (f32[8,16,16]{2,1,0:T(8,128)S(1)}, f32[8,16,16]{2,1,0:T(8,128)}, u32[]{:S(2)}) copy-start(f32[8,16,16]{2,1,0:T(8,128)} %mul.434) | copy-start | bytes 24580
  951.9 13.7 %copy-start.41 = (f32[8,16,16]{2,1,0:T(8,128)S(1)}, f32[8,16,16]{2,1,0:T(8,128)}, u32[]{:S(2)}) copy-start(f32[8,16,16]{2,1,0:T(8,128)} %mul.431) | copy-start | bytes 24580
  952.0 1.4 collective-permute-start.11
  954.1 6.1 collective-permute-start.12
  959.0 36.4 %collective-permute-start.7 = (bf16[4,256,3,1,128]{4,3,2,1,0:T(2,128)(2,1)S(1)}, bf16[4,256,3,1,128]{4,3,2,1,0:T(2,128)(2,1)}, u32[]{:S(2)}, u32[]{:S(2)}) collective-permute-start(bf16[4,256,3,1,128]{4,3,2,1,0:T(2,128)(2,1)S(1)} %copy.72), channel_id=1, source_target_pairs={{0,64},{32,96},{64,0},{96,32},{1,65},{33,97},{65,1},{97,33},{2,66}... | collective-permute-start | bytes 2359304 | tf_op jit(solution)/shard_map/ppermute | solution.py:350
  966.7 33.0 %collective-permute-start = (f32[8,8,192]{2,0,1:T(8,128)S(1)}, f32[8,8,192]{2,0,1:T(8,128)S(1)}, u32[]{:S(2)}, u32[]{:S(2)}) collective-permute-start(f32[8,8,192]{2,0,1:T(8,128)S(1)} %slice_select_fusion.2), channel_id=1, source_target_pairs={{0,8},{1,9},{2,10},{3,11},{4,12},{5,13},{6,14},{7,15},{8,0},{9,1},... | collective-permute-start | bytes 147464 | tf_op jit(solution)/shard_map/ppermute | solution.py:350
  999.7 24.2 %copy-start.20 = (f32[128,1,2048]{2,0,1:T(8,128)S(1)}, f32[128,1,2048]{2,0,1:T(8,128)}, u32[]{:S(2)}) copy-start(f32[128,1,2048]{2,0,1:T(8,128)} %copy-done.19) | copy-start | bytes 3145732
  999.7 24.2 %copy-start.22 = (bf16[128,1,2048]{2,0,1:T(8,128)(2,1)S(1)}, bf16[128,1,2048]{2,0,1:T(8,128)(2,1)}, u32[]{:S(2)}) copy-start(bf16[128,1,2048]{2,0,1:T(8,128)(2,1)} %get-tuple-element.79) | copy-start | bytes 1572868
  999.7 24.2 %copy-start.23 = (bf16[128,1,2048]{2,0,1:T(8,128)(2,1)S(1)}, bf16[128,1,2048]{2,0,1:T(8,128)(2,1)}, u32[]{:S(2)}) copy-start(bf16[128,1,2048]{2,0,1:T(8,128)(2,1)} %reduce-scatter.11.cloned.1.call-done) | copy-start | bytes 1572868
  999.7 24.2 %copy-start.65 = (f32[128]{0:T(128)S(1)}, f32[128]{0:T(128)}, u32[]{:S(2)}) copy-start(f32[128]{0:T(128)} %copy-done.64) | copy-start | bytes 1540
  999.8 4.0 collective-permute-start.1
  1002.1 4.8 collective-permute-start.8
  1003.8 26.2 %copy-start.1 = (bf16[512,2048]{1,0:T(8,128)(2,1)S(1)}, bf16[512,2048]{1,0:T(8,128)(2,1)}, u32[]{:S(2)}) copy-start(bf16[512,2048]{1,0:T(8,128)(2,1)} %param.28) | copy-start | bytes 6291460
  1003.8 5.3 collective-permute-start.2
  1009.2 3.7 collective-permute-start.3
  1011.1 9.4 collective-permute-start.9
  1012.9 8.9 collective-permute-start.4
  1021.9 1.2 collective-permute-start.5
  1023.1 5.2 collective-permute-start.6
  (40 other events, 161.3 us)
Sparse Core Ops, SparseCore 0:
  224.4 114.1 reduce-scatter.4
  341.7 70.2 all-gather.3
  414.7 70.3 all-gather.5
  507.4 110.2 reduce-scatter.8
  621.0 84.5 reduce-scatter.6
  709.4 69.9 all-gather.7
  843.9 84.3 reduce-scatter.10
